TPU v7x, 32 devices: a whole 2x2x4 slice. The times are simulated.
32 devices in a mesh: ev: 4 (over y, x), co: 8 (over z, core).
Axes of the slice: x: 2, y: 2, z: 4, core: 2. Of those that a mesh axis runs over, the one named last changes fastest.
Arguments:
- eval_points: float32 [2048, 1024], P('ev', 'co'), may hold values from -7 to 7
- corpus_points: float32 [4096, 1024], P('co', 'ev'), may hold values from -7 to 7
Outputs:
- eval_mapped: float32 [2048, 1024], P(('ev', 'co'))
- corpus_mapped: float32 [4096, 1024], P(('co', 'ev'))
- eval_potential: float32 [2048], P('ev')
- corpus_potential: float32 [4096], P('co')
All inputs are finite; a program needn't handle non-finite values.
Results may differ from a plain program's by a relative error of at most 0.0003.
Values sent between devices are 32-bit elements; how exact they have to be, the bound alone decides.
No kernel may reach another device: no remote copies, remote signals or barrier semaphores. Data moves between devices by JAX's collectives and lax.ppermute only.
A program may use at most 64 MiB of HBM per device.

v0:
```python
import math
import jax
import jax.numpy as jnp
from jax import lax
from jax.sharding import PartitionSpec as P

ITERS = 3
EPSILON = 0.02


def row_reduce(scores):
    largest = lax.pmax(jnp.max(scores, axis=1), "co")
    summed = lax.psum(jnp.sum(jnp.exp(scores - largest[:, None]), axis=1), "co")
    return largest + jnp.log(summed)


def column_reduce(scores):
    largest = lax.pmax(jnp.max(scores, axis=0), "ev")
    summed = lax.psum(jnp.sum(jnp.exp(scores - largest[None, :]), axis=0), "ev")
    return largest + jnp.log(summed)


def on_device(eval_points, corpus_points):
    eval_full = lax.all_gather(eval_points, "co", axis=1, tiled=True)
    corpus_full = lax.all_gather(corpus_points, "ev", axis=1, tiled=True)
    embed_width = eval_full.shape[1]
    eval_rows_here = eval_full.shape[0]
    corpus_rows_here = corpus_full.shape[0]
    eval_norms = jnp.sum(eval_full * eval_full, axis=1)
    corpus_norms = jnp.sum(corpus_full * corpus_full, axis=1)
    cross_term = lax.dot_general(
        eval_full,
        corpus_full,
        (((1,), (1,)), ((), ())),
        precision=lax.Precision.HIGHEST,
        preferred_element_type=jnp.float32,
    )
    cost_tile = (eval_norms[:, None] + corpus_norms[None, :] - 2.0 * cross_term) / embed_width
    log_mass_x = -math.log(eval_rows_here * lax.axis_size("ev"))
    log_mass_y = -math.log(corpus_rows_here * lax.axis_size("co"))
    corpus_potential = jnp.zeros((corpus_rows_here,), jnp.float32)
    eval_potential = jnp.zeros((eval_rows_here,), jnp.float32)
    column_lse = jnp.zeros((corpus_rows_here,), jnp.float32)
    for sweep in range(ITERS):
        eval_potential = EPSILON * log_mass_x - EPSILON * row_reduce(
            (corpus_potential[None, :] - cost_tile) / EPSILON
        )
        column_lse = column_reduce((eval_potential[:, None] - cost_tile) / EPSILON)
        corpus_potential = EPSILON * log_mass_y - EPSILON * column_lse
    row_scores = (corpus_potential[None, :] - cost_tile) / EPSILON
    row_final = row_reduce(row_scores)
    x_weights = jnp.exp(row_scores - row_final[:, None])
    y_weights = jnp.exp((eval_potential[:, None] - cost_tile) / EPSILON - column_lse[None, :])
    eval_portion = eval_rows_here // lax.axis_size("co")
    corpus_portion = corpus_rows_here // lax.axis_size("ev")
    eval_whole = lax.psum(
        jnp.dot(
            x_weights,
            corpus_full,
            precision=lax.Precision.HIGHEST,
            preferred_element_type=jnp.float32,
        ),
        "co",
    )
    eval_mapped = lax.dynamic_slice_in_dim(
        eval_whole, lax.axis_index("co") * eval_portion, eval_portion, 0
    )
    corpus_whole = lax.psum(
        lax.dot_general(
            y_weights,
            eval_full,
            (((0,), (0,)), ((), ())),
            precision=lax.Precision.HIGHEST,
            preferred_element_type=jnp.float32,
        ),
        "ev",
    )
    corpus_mapped = lax.dynamic_slice_in_dim(
        corpus_whole, lax.axis_index("ev") * corpus_portion, corpus_portion, 0
    )
    return (eval_mapped, corpus_mapped, eval_potential, corpus_potential)


def solution(mesh):
    return jax.shard_map(
        on_device,
        mesh=mesh,
        in_specs=(P("ev", "co"), P("co", "ev")),
        out_specs=(P(("ev", "co"), None), P(("co", "ev"), None), P("ev"), P("co")),
        check_vma=False,
    )
```

profile of v0, /device:TPU:0, one launch (start us, length us, event | category | flops | bytes accessed | tf_op | source)
XLA Modules:
  0.0 402.7 jit_solution(11580562035312016209)
XLA Ops:
  8.7 38.9 %all-gather.5.cloned.1.call-done = f32[512,1024]{1,0:T(8,128)} async-done(((f32[512,256]{1,0:T(8,128)}), f32[512,1024]{1,0:T(8,128)}) %all-gather.5.cloned.1.call-update) | async-done | bytes 2097168 | tf_op jit(solution)/shard_map/all_gather | solution.py:25
  47.6 1.8 multiply_reduce_fusion
  49.4 30.4 %all-gather.3.cloned.1.call-done = f32[512,1024]{1,0:T(8,128)} async-done(((f32[512,128]{1,0:T(8,128)}), f32[512,1024]{1,0:T(8,128)}) %all-gather.3.cloned.1.call-update) | async-done | bytes 2097168 | tf_op jit(solution)/shard_map/all_gather | solution.py:24
  79.8 2.0 multiply_reduce_fusion.1
  82.1 5.2 %fusion.8 = (f32[512]{0:T(512)S(1)}, f32[512,512]{0,1:T(8,128)S(1)}) fusion(f32[512,1024]{1,0:T(8,128)S(1)} %copy-done, f32[512,1024]{1,0:T(8,128)} %all-gather.5.cloned.1.call-done, f32[512]{0:T(512)S(1)} %multiply_reduce_fusion, f32[512]{0:T(512)S(1)} %multiply_reduce_fusion.1), kind=kOutput, calls=%fused_computation.25 | convolution fusion | flops 3223059968 | bytes 5249024 | tf_op jit(solution)/shard_map/dot_general | solution.py:31
  87.3 14.5 %pmax.49 = f32[512]{0:T(512)S(1)} all-reduce(f32[512]{0:T(512)S(1)} %get-tuple-element.6), channel_id=1, replica_groups=mesh['ev'=4,'co'=8] {'co'}, use_global_device_ids=true, to_apply=%region_3.0 | all-reduce | flops 512 | bytes 4096 | tf_op jit(solution)/shard_map/pmax | solution.py:12
  102.0 13.6 %psum.63 = f32[512]{0:T(512)S(1)} all-reduce(f32[512]{0:T(512)S(1)} %exponential_reduce_fusion.6), channel_id=1, replica_groups=mesh['ev'=4,'co'=8] {'co'}, use_global_device_ids=true, to_apply=%region_5.0 | all-reduce | flops 512 | bytes 4096 | tf_op jit(solution)/shard_map/psum | solution.py:13
  115.8 9.8 %pmax.50 = f32[512]{0:T(512)S(1)} all-reduce(f32[512]{0:T(512)S(1)} %fusion.9), channel_id=1, replica_groups=mesh['ev'=4,'co'=8] {'ev'}, use_global_device_ids=true, to_apply=%region_7.0 | all-reduce | flops 512 | bytes 4096 | tf_op jit(solution)/shard_map/pmax | solution.py:18
  125.9 8.0 %psum.64 = f32[512]{0:T(512)S(1)} all-reduce(f32[512]{0:T(512)S(1)} %exponential_reduce_fusion.5), channel_id=1, replica_groups=mesh['ev'=4,'co'=8] {'ev'}, use_global_device_ids=true, to_apply=%region_9.0 | all-reduce | flops 512 | bytes 4096 | tf_op jit(solution)/shard_map/psum | solution.py:19
  134.2 13.6 %pmax.51 = f32[512]{0:T(512)S(1)} all-reduce(f32[512]{0:T(512)S(1)} %fusion.10), channel_id=1, replica_groups=mesh['ev'=4,'co'=8] {'co'}, use_global_device_ids=true, to_apply=%region_11.0 | all-reduce | flops 512 | bytes 4096 | tf_op jit(solution)/shard_map/pmax | solution.py:12
  148.1 13.6 %psum.65 = f32[512]{0:T(512)S(1)} all-reduce(f32[512]{0:T(512)S(1)} %exponential_reduce_fusion.4), channel_id=1, replica_groups=mesh['ev'=4,'co'=8] {'co'}, use_global_device_ids=true, to_apply=%region_13.0 | all-reduce | flops 512 | bytes 4096 | tf_op jit(solution)/shard_map/psum | solution.py:13
  161.9 8.9 %pmax.52 = f32[512]{0:T(512)S(1)} all-reduce(f32[512]{0:T(512)S(1)} %fusion.11), channel_id=1, replica_groups=mesh['ev'=4,'co'=8] {'ev'}, use_global_device_ids=true, to_apply=%region_15.0 | all-reduce | flops 512 | bytes 4096 | tf_op jit(solution)/shard_map/pmax | solution.py:18
  171.1 8.0 %psum.66 = f32[512]{0:T(512)S(1)} all-reduce(f32[512]{0:T(512)S(1)} %exponential_reduce_fusion.3), channel_id=1, replica_groups=mesh['ev'=4,'co'=8] {'ev'}, use_global_device_ids=true, to_apply=%region_17.0 | all-reduce | flops 512 | bytes 4096 | tf_op jit(solution)/shard_map/psum | solution.py:19
  179.4 13.6 %pmax.53 = f32[512]{0:T(512)S(1)} all-reduce(f32[512]{0:T(512)S(1)} %fusion.12), channel_id=1, replica_groups=mesh['ev'=4,'co'=8] {'co'}, use_global_device_ids=true, to_apply=%region_19.0 | all-reduce | flops 512 | bytes 4096 | tf_op jit(solution)/shard_map/pmax | solution.py:12
  193.3 13.6 %psum.67 = f32[512]{0:T(512)S(1)} all-reduce(f32[512]{0:T(512)S(1)} %exponential_reduce_fusion.2), channel_id=1, replica_groups=mesh['ev'=4,'co'=8] {'co'}, use_global_device_ids=true, to_apply=%region_21.0 | all-reduce | flops 512 | bytes 4096 | tf_op jit(solution)/shard_map/psum | solution.py:13
  207.1 9.7 %pmax.54 = f32[512]{0:T(512)S(1)} all-reduce(f32[512]{0:T(512)S(1)} %fusion.13), channel_id=1, replica_groups=mesh['ev'=4,'co'=8] {'ev'}, use_global_device_ids=true, to_apply=%region_23.0 | all-reduce | flops 512 | bytes 4096 | tf_op jit(solution)/shard_map/pmax | solution.py:18
  217.1 8.0 %psum.68 = f32[512]{0:T(512)S(1)} all-reduce(f32[512]{0:T(512)S(1)} %exponential_reduce_fusion.1), channel_id=1, replica_groups=mesh['ev'=4,'co'=8] {'ev'}, use_global_device_ids=true, to_apply=%region_25.0 | all-reduce | flops 512 | bytes 4096 | tf_op jit(solution)/shard_map/psum | solution.py:19
  225.4 13.6 %pmax.55 = f32[512]{0:T(512)S(1)} all-reduce(f32[512]{0:T(512)S(1)} %fusion.14), channel_id=1, replica_groups=mesh['ev'=4,'co'=8] {'co'}, use_global_device_ids=true, to_apply=%region_27.0 | all-reduce | flops 512 | bytes 4096 | tf_op jit(solution)/shard_map/pmax | solution.py:12
  239.2 13.8 %psum.69 = f32[512]{0:T(512)S(1)} all-reduce(f32[512]{0:T(512)S(1)} %exponential_reduce_fusion), channel_id=1, replica_groups=mesh['ev'=4,'co'=8] {'co'}, use_global_device_ids=true, to_apply=%region_29.0 | all-reduce | flops 512 | bytes 4096 | tf_op jit(solution)/shard_map/psum | solution.py:13
  253.0 6.6 %fusion.5 = f32[512,1024]{1,0:T(8,128)} fusion(f32[512,1024]{1,0:T(8,128)} %all-gather.5.cloned.1.call-done, f32[512,512]{0,1:T(8,128)S(1)} %get-tuple-element.7, f32[512]{0:T(512)S(1)} %log_add_fusion, f32[512]{0:T(512)S(1)} %get-tuple-element.4), kind=kOutput, calls=%fused_computation.8 | convolution fusion | flops 3222011904 | bytes 5246976 | tf_op jit(solution)/shard_map/dot_general | solution.py:57
  259.7 5.0 %fusion.2 = f32[512,1024]{1,0:T(8,128)} fusion(f32[512,1024]{1,0:T(8,128)S(1)} %copy-done, f32[512,512]{0,1:T(8,128)S(1)} %get-tuple-element.7, f32[512]{0:T(512)S(1)} %get-tuple-element.5, f32[512]{0:T(512)S(1)} %multiply_subtract_fusion.1), kind=kOutput, calls=%fused_computation.5 | convolution fusion | flops 3222011904 | bytes 5246976 | tf_op jit(solution)/shard_map/dot_general | solution.py:69
  264.7 57.5 %all-reduce.3.cloned.1.call-done = f32[512,1024]{1,0:T(8,128)} async-done(((f32[512,1024]{1,0:T(8,128)}), f32[512,1024]{1,0:T(8,128)}) %all-reduce.3.cloned.1.call-update) | async-done | bytes 2097168 | tf_op jit(solution)/shard_map/psum | solution.py:56
  323.9 70.4 %all-reduce.5.cloned.1.call-done = f32[512,1024]{1,0:T(8,128)} async-done(((f32[512,1024]{1,0:T(8,128)}), f32[512,1024]{1,0:T(8,128)}) %all-reduce.5.cloned.1.call-update) | async-done | bytes 2097168 | tf_op jit(solution)/shard_map/psum | solution.py:68
  394.3 1.9 constant_dynamic-slice_fusion
  (35 shorter events, 6.8 us)
Async XLA Ops:
  7.2 40.4 %all-gather.5.cloned.1.call-start = ((), (), s32[]{:S(2)}) async-start(), calls=%async_computation.1 | async-start | bytes 2621440 | tf_op jit(solution)/shard_map/all_gather | solution.py:25
  7.9 71.9 %all-gather.3.cloned.1.call-start = ((), (), s32[]{:S(2)}) async-start(), calls=%async_computation | async-start | bytes 2359296 | tf_op jit(solution)/shard_map/all_gather | solution.py:24
  8.6 313.5 %all-reduce.3.cloned.1.call-start = ((), (), s32[]{:S(2)}) async-start(), calls=%async_computation.2 | async-start | bytes 4194304 | tf_op jit(solution)/shard_map/psum | solution.py:56
  79.8 2.2 copy-start
  206.9 52.8 %copy-start.1 = (f32[512]{0:T(512)}, f32[512]{0:T(512)S(1)}, u32[]{:S(2)}) copy-start(f32[512]{0:T(512)S(1)} %multiply_subtract_fusion.1) | copy-start | bytes 6148
  225.2 34.4 %copy-start.2 = (f32[512]{0:T(512)}, f32[512]{0:T(512)S(1)}, u32[]{:S(2)}) copy-start(f32[512]{0:T(512)S(1)} %get-tuple-element.4) | copy-start | bytes 6148
  259.6 134.6 %all-reduce.5.cloned.1.call-start = ((), (), s32[]{:S(2)}) async-start(), calls=%async_computation.3 | async-start | bytes 4194304 | tf_op jit(solution)/shard_map/psum | solution.py:68
Sparse Core Ops, SparseCore 0:
  9.8 37.7 all-gather.4
  49.2 30.5 all-gather.2
  259.7 62.3 all-reduce.2
  325.1 69.0 all-reduce.4
where the time goes:
time: 403 us
  waiting for transfers between devices  199 us (49%)
  blocking collectives  162 us (40%)
  matrix products  16.8 us (4%)
  between operations  13.8 us (3%)
  other arithmetic  7.07 us (2%)
    psum x1, waiting for transfers between devices, on_device(): lax.psum(lax.dot_general(y_weights, eval_full, (((0,), (0,)), ((), ())),...  70.4 us
    psum x1, waiting for transfers between devices, on_device(): lax.psum(jnp.dot(x_weights, corpus_full, precision=lax.Precision.HIGHEST,...  57.5 us
    pmax x4, blocking collectives, row_reduce(): largest = lax.pmax(jnp.max(scores, axis=1), 'co')  55.3 us
    psum x4, blocking collectives, row_reduce(): summed = lax.psum(jnp.sum(jnp.exp(scores - largest[:, None]), axis=1), 'co')  54.6 us
    all_gather x1, waiting for transfers between devices, on_device(): corpus_full = lax.all_gather(corpus_points, 'ev', axis=1, tiled=True)  38.9 us
    all_gather x1, waiting for transfers between devices, on_device(): eval_full = lax.all_gather(eval_points, 'co', axis=1, tiled=True)  30.4 us
    pmax x3, blocking collectives, column_reduce(): largest = lax.pmax(jnp.max(scores, axis=0), 'ev')  28.4 us
    psum x3, blocking collectives, column_reduce(): summed = lax.psum(jnp.sum(jnp.exp(scores - largest[None, :]), axis=0), 'ev')  24.1 us
  transfers between devices with their start and end apart: 4, of which 4 were waited for; matrix products, arithmetic and copies ran while one was open for 2% of the time, Pallas kernels for 0%

commit v1 on v0

--- a/solution.py
+++ b/solution.py
@@ -6,6 +6,16 @@
 
 ITERS = 3
 EPSILON = 0.02
+
+
+def gather_around(x, axis, dim):
+    ways, here, step = (lax.axis_size(axis), lax.axis_index(axis), x.shape[dim])
+    shape = [n * ways if d == dim else n for d, n in enumerate(x.shape)]
+    full = lax.dynamic_update_slice_in_dim(jnp.zeros(shape, x.dtype), x, here * step, axis=dim)
+    for far in range(1, ways):
+        x = lax.ppermute(x, axis, [(d, (d + 1) % ways) for d in range(ways)])
+        full = lax.dynamic_update_slice_in_dim(full, x, (here - far) % ways * step, axis=dim)
+    return full
 
 
 def row_reduce(scores):
@@ -21,7 +31,7 @@
 
 
 def on_device(eval_points, corpus_points):
-    eval_full = lax.all_gather(eval_points, "co", axis=1, tiled=True)
+    eval_full = gather_around(eval_points, "co", 1)
     corpus_full = lax.all_gather(corpus_points, "ev", axis=1, tiled=True)
     embed_width = eval_full.shape[1]
     eval_rows_here = eval_full.shape[0]

time: 403 us -> 384 us (0.953)
  waiting for transfers between devices: 199 us -> 182 us
    ppermute x0 -> x7, waiting for transfers between devices: none -> 53.4 us  [gather_around(): x = lax.ppermute(x, axis, [(d, (d + 1) % ways) for d in range(ways)])]
    all_gather x1, waiting for transfers between devices: 38.9 us -> 0.02 us  [on_device(): corpus_full = lax.all_gather(corpus_points, 'ev', axis=1, tiled=True)]
    all_gather x1 -> x0, waiting for transfers between devices: 30.4 us -> none  [on_device(): eval_full = lax.all_gather(eval_points, 'co', axis=1, tiled=True)]
  transfers between devices with their start and end apart: 4 -> 10, of which waited for: 4 -> 9; matrix products, arithmetic and copies ran while one was open for 2% -> 2% of each run, Pallas kernels for 0% -> 0%
where the time goes in v1:
time: 384 us
  waiting for transfers between devices  182 us (47%)
  blocking collectives  162 us (42%)
  matrix products  15.3 us (4%)
  between operations  13.9 us (4%)
  other arithmetic  5.48 us (1%)
  local copies, waits for them, and re-layouts  4.3 us (1%)
    psum x1, waiting for transfers between devices, on_device(): lax.psum(lax.dot_general(y_weights, eval_full, (((0,), (0,)), ((), ())),...  70.6 us
    psum x1, waiting for transfers between devices, on_device(): lax.psum(jnp.dot(x_weights, corpus_full, precision=lax.Precision.HIGHEST,...  57.5 us
    psum x4, blocking collectives, row_reduce(): summed = lax.psum(jnp.sum(jnp.exp(scores - largest[:, None]), axis=1), 'co')  54.6 us
    pmax x4, blocking collectives, row_reduce(): largest = lax.pmax(jnp.max(scores, axis=1), 'co')  54.4 us
    ppermute x7, waiting for transfers between devices, gather_around(): x = lax.ppermute(x, axis, [(d, (d + 1) % ways) for d in range(ways)])  53.4 us
    pmax x3, blocking collectives, column_reduce(): largest = lax.pmax(jnp.max(scores, axis=0), 'ev')  29.1 us
    psum x3, blocking collectives, column_reduce(): summed = lax.psum(jnp.sum(jnp.exp(scores - largest[None, :]), axis=0), 'ev')  24.1 us
  transfers between devices with their start and end apart: 10, of which 9 were waited for; matrix products, arithmetic and copies ran while one was open for 2% of the time, Pallas kernels for 0%

profile of v1, /device:TPU:0, one launch (start us, length us, event | category | flops | bytes accessed | tf_op | source)
XLA Modules:
  0.0 383.9 jit_solution(2967165605155588895)
XLA Ops:
  8.5 8.3 %collective-permute-done = f32[512,128]{1,0:T(8,128)S(1)} collective-permute-done((f32[512,128]{1,0:T(8,128)}, f32[512,128]{1,0:T(8,128)S(1)}, u32[]{:S(2)}, u32[]{:S(2)}) %collective-permute-start) | collective-permute-done | bytes 262176 | tf_op jit(solution)/shard_map/ppermute | solution.py:16
  16.8 7.6 %collective-permute-done.1 = f32[512,128]{1,0:T(8,128)S(1)} collective-permute-done((f32[512,128]{1,0:T(8,128)S(1)}, f32[512,128]{1,0:T(8,128)S(1)}, u32[]{:S(2)}, u32[]{:S(2)}) %collective-permute-start.1) | collective-permute-done | bytes 262176 | tf_op jit(solution)/shard_map/ppermute | solution.py:16
  24.4 7.6 %collective-permute-done.2 = f32[512,128]{1,0:T(8,128)S(1)} collective-permute-done((f32[512,128]{1,0:T(8,128)S(1)}, f32[512,128]{1,0:T(8,128)S(1)}, u32[]{:S(2)}, u32[]{:S(2)}) %collective-permute-start.2) | collective-permute-done | bytes 262176 | tf_op jit(solution)/shard_map/ppermute | solution.py:16
  32.0 7.6 %collective-permute-done.3 = f32[512,128]{1,0:T(8,128)S(1)} collective-permute-done((f32[512,128]{1,0:T(8,128)S(1)}, f32[512,128]{1,0:T(8,128)S(1)}, u32[]{:S(2)}, u32[]{:S(2)}) %collective-permute-start.3) | collective-permute-done | bytes 262176 | tf_op jit(solution)/shard_map/ppermute | solution.py:16
  39.9 7.3 %collective-permute-done.4 = f32[512,128]{1,0:T(8,128)S(1)} collective-permute-done((f32[512,128]{1,0:T(8,128)S(1)}, f32[512,128]{1,0:T(8,128)S(1)}, u32[]{:S(2)}, u32[]{:S(2)}) %collective-permute-start.4) | collective-permute-done | bytes 262176 | tf_op jit(solution)/shard_map/ppermute | solution.py:16
  47.3 7.5 %collective-permute-done.5 = f32[512,128]{1,0:T(8,128)S(1)} collective-permute-done((f32[512,128]{1,0:T(8,128)S(1)}, f32[512,128]{1,0:T(8,128)S(1)}, u32[]{:S(2)}, u32[]{:S(2)}) %collective-permute-start.5) | collective-permute-done | bytes 262176 | tf_op jit(solution)/shard_map/ppermute | solution.py:16
  54.9 7.5 %collective-permute-done.6 = f32[512,128]{1,0:T(8,128)S(1)} collective-permute-done((f32[512,128]{1,0:T(8,128)S(1)}, f32[512,128]{1,0:T(8,128)S(1)}, u32[]{:S(2)}, u32[]{:S(2)}) %collective-permute-start.6) | collective-permute-done | bytes 262176 | tf_op jit(solution)/shard_map/ppermute | solution.py:16
  68.7 13.6 %pmax.49 = f32[512]{0:T(512)S(1)} all-reduce(f32[512]{0:T(512)S(1)} %get-tuple-element.6), channel_id=1, replica_groups=mesh['ev'=4,'co'=8] {'co'}, use_global_device_ids=true, to_apply=%region_3.4 | all-reduce | flops 512 | bytes 4096 | tf_op jit(solution)/shard_map/pmax | solution.py:22
  82.5 13.6 %psum.63 = f32[512]{0:T(512)S(1)} all-reduce(f32[512]{0:T(512)S(1)} %exponential_reduce_fusion.6), channel_id=1, replica_groups=mesh['ev'=4,'co'=8] {'co'}, use_global_device_ids=true, to_apply=%region_5.6 | all-reduce | flops 512 | bytes 4096 | tf_op jit(solution)/shard_map/psum | solution.py:23
  96.3 10.4 %pmax.50 = f32[512]{0:T(512)S(1)} all-reduce(f32[512]{0:T(512)S(1)} %fusion.7), channel_id=1, replica_groups=mesh['ev'=4,'co'=8] {'ev'}, use_global_device_ids=true, to_apply=%region_7.8 | all-reduce | flops 512 | bytes 4096 | tf_op jit(solution)/shard_map/pmax | solution.py:28
  107.0 8.0 %psum.64 = f32[512]{0:T(512)S(1)} all-reduce(f32[512]{0:T(512)S(1)} %exponential_reduce_fusion.5), channel_id=1, replica_groups=mesh['ev'=4,'co'=8] {'ev'}, use_global_device_ids=true, to_apply=%region_9.10 | all-reduce | flops 512 | bytes 4096 | tf_op jit(solution)/shard_map/psum | solution.py:29
  115.2 13.6 %pmax.51 = f32[512]{0:T(512)S(1)} all-reduce(f32[512]{0:T(512)S(1)} %fusion.8), channel_id=1, replica_groups=mesh['ev'=4,'co'=8] {'co'}, use_global_device_ids=true, to_apply=%region_11.12 | all-reduce | flops 512 | bytes 4096 | tf_op jit(solution)/shard_map/pmax | solution.py:22
  129.1 13.6 %psum.65 = f32[512]{0:T(512)S(1)} all-reduce(f32[512]{0:T(512)S(1)} %exponential_reduce_fusion.4), channel_id=1, replica_groups=mesh['ev'=4,'co'=8] {'co'}, use_global_device_ids=true, to_apply=%region_13.14 | all-reduce | flops 512 | bytes 4096 | tf_op jit(solution)/shard_map/psum | solution.py:23
  142.9 9.0 %pmax.52 = f32[512]{0:T(512)S(1)} all-reduce(f32[512]{0:T(512)S(1)} %fusion.9), channel_id=1, replica_groups=mesh['ev'=4,'co'=8] {'ev'}, use_global_device_ids=true, to_apply=%region_15.16 | all-reduce | flops 512 | bytes 4096 | tf_op jit(solution)/shard_map/pmax | solution.py:28
  152.2 8.0 %psum.66 = f32[512]{0:T(512)S(1)} all-reduce(f32[512]{0:T(512)S(1)} %exponential_reduce_fusion.3), channel_id=1, replica_groups=mesh['ev'=4,'co'=8] {'ev'}, use_global_device_ids=true, to_apply=%region_17.18 | all-reduce | flops 512 | bytes 4096 | tf_op jit(solution)/shard_map/psum | solution.py:29
  160.5 13.6 %pmax.53 = f32[512]{0:T(512)S(1)} all-reduce(f32[512]{0:T(512)S(1)} %fusion.10), channel_id=1, replica_groups=mesh['ev'=4,'co'=8] {'co'}, use_global_device_ids=true, to_apply=%region_19.20 | all-reduce | flops 512 | bytes 4096 | tf_op jit(solution)/shard_map/pmax | solution.py:22
  174.3 13.6 %psum.67 = f32[512]{0:T(512)S(1)} all-reduce(f32[512]{0:T(512)S(1)} %exponential_reduce_fusion.2), channel_id=1, replica_groups=mesh['ev'=4,'co'=8] {'co'}, use_global_device_ids=true, to_apply=%region_21.22 | all-reduce | flops 512 | bytes 4096 | tf_op jit(solution)/shard_map/psum | solution.py:23
  188.1 9.7 %pmax.54 = f32[512]{0:T(512)S(1)} all-reduce(f32[512]{0:T(512)S(1)} %fusion.11), channel_id=1, replica_groups=mesh['ev'=4,'co'=8] {'ev'}, use_global_device_ids=true, to_apply=%region_23.24 | all-reduce | flops 512 | bytes 4096 | tf_op jit(solution)/shard_map/pmax | solution.py:28
  198.2 8.0 %psum.68 = f32[512]{0:T(512)S(1)} all-reduce(f32[512]{0:T(512)S(1)} %exponential_reduce_fusion.1), channel_id=1, replica_groups=mesh['ev'=4,'co'=8] {'ev'}, use_global_device_ids=true, to_apply=%region_25.26 | all-reduce | flops 512 | bytes 4096 | tf_op jit(solution)/shard_map/psum | solution.py:29
  206.4 13.6 %pmax.55 = f32[512]{0:T(512)S(1)} all-reduce(f32[512]{0:T(512)S(1)} %fusion.12), channel_id=1, replica_groups=mesh['ev'=4,'co'=8] {'co'}, use_global_device_ids=true, to_apply=%region_27.28 | all-reduce | flops 512 | bytes 4096 | tf_op jit(solution)/shard_map/pmax | solution.py:22
  220.3 13.8 %psum.69 = f32[512]{0:T(512)S(1)} all-reduce(f32[512]{0:T(512)S(1)} %exponential_reduce_fusion), channel_id=1, replica_groups=mesh['ev'=4,'co'=8] {'co'}, use_global_device_ids=true, to_apply=%region_29.30 | all-reduce | flops 512 | bytes 4096 | tf_op jit(solution)/shard_map/psum | solution.py:23
  234.1 6.6 %fusion.3 = f32[512,1024]{1,0:T(8,128)} fusion(f32[512,1024]{1,0:T(8,128)} %all-gather.2.cloned.1.call-done, f32[512,512]{0,1:T(8,128)S(1)} %get-tuple-element.7, f32[512]{0:T(512)S(1)} %log_add_fusion, f32[512]{0:T(512)S(1)} %get-tuple-element.4), kind=kOutput, calls=%fused_computation.6 | convolution fusion | flops 3222011904 | bytes 5246976 | tf_op jit(solution)/shard_map/dot_general | solution.py:67
  245.8 57.5 %all-reduce.3.cloned.1.call-done = f32[512,1024]{1,0:T(8,128)} async-done(((f32[512,1024]{1,0:T(8,128)}), f32[512,1024]{1,0:T(8,128)}) %all-reduce.3.cloned.1.call-update) | async-done | bytes 2097168 | tf_op jit(solution)/shard_map/psum | solution.py:66
  304.9 70.6 %all-reduce.5.cloned.1.call-done = f32[512,1024]{1,0:T(8,128)} async-done(((f32[512,1024]{1,0:T(8,128)}), f32[512,1024]{1,0:T(8,128)}) %all-reduce.5.cloned.1.call-update) | async-done | bytes 2097168 | tf_op jit(solution)/shard_map/psum | solution.py:78
  (61 shorter events, 19.9 us)
Async XLA Ops:
  7.2 32.7 %copy-start.1 = (f32[512,128]{1,0:T(8,128)S(1)}, f32[512,128]{1,0:T(8,128)}, u32[]{:S(2)}) copy-start(f32[512,128]{1,0:T(8,128)} %param.2) | copy-start | bytes 786436
  7.2 55.5 %all-gather.2.cloned.1.call-start = ((), (), s32[]{:S(2)}) async-start(), calls=%async_computation | async-start | bytes 2621440 | tf_op jit(solution)/shard_map/all_gather | solution.py:35
  7.9 295.3 %all-reduce.3.cloned.1.call-start = ((), (), s32[]{:S(2)}) async-start(), calls=%async_computation.1 | async-start | bytes 4194304 | tf_op jit(solution)/shard_map/psum | solution.py:66
  8.0 8.8 %collective-permute-start = (f32[512,128]{1,0:T(8,128)}, f32[512,128]{1,0:T(8,128)S(1)}, u32[]{:S(2)}, u32[]{:S(2)}) collective-permute-start(f32[512,128]{1,0:T(8,128)} %param.2), channel_id=1, source_target_pairs={{0,1},{1,2},{2,3},{3,4},{4,5},{5,6},{6,7},{7,0},{8,9},{9,10},{10,1... | collective-permute-start | bytes 786440 | tf_op jit(solution)/shard_map/ppermute | solution.py:16
  16.8 7.6 %collective-permute-start.1 = (f32[512,128]{1,0:T(8,128)S(1)}, f32[512,128]{1,0:T(8,128)S(1)}, u32[]{:S(2)}, u32[]{:S(2)}) collective-permute-start(f32[512,128]{1,0:T(8,128)S(1)} %collective-permute-done), channel_id=1, source_target_pairs={{0,1},{1,2},{2,3},{3,4},{4,5},{5,6},{6,7},{7,0},{8,9},{9,10},{10,1... | collective-permute-start | bytes 786440 | tf_op jit(solution)/shard_map/ppermute | solution.py:16
  24.4 7.6 %collective-permute-start.2 = (f32[512,128]{1,0:T(8,128)S(1)}, f32[512,128]{1,0:T(8,128)S(1)}, u32[]{:S(2)}, u32[]{:S(2)}) collective-permute-start(f32[512,128]{1,0:T(8,128)S(1)} %collective-permute-done.1), channel_id=1, source_target_pairs={{0,1},{1,2},{2,3},{3,4},{4,5},{5,6},{6,7},{7,0},{8,9},{9,10},{10,1... | collective-permute-start | bytes 786440 | tf_op jit(solution)/shard_map/ppermute | solution.py:16
  32.0 7.6 %copy-start.2 = (f32[512,128]{1,0:T(8,128)}, f32[512,128]{1,0:T(8,128)S(1)}, u32[]{:S(2)}) copy-start(f32[512,128]{1,0:T(8,128)S(1)} %collective-permute-done.2) | copy-start | bytes 786436
  32.0 7.6 %collective-permute-start.3 = (f32[512,128]{1,0:T(8,128)S(1)}, f32[512,128]{1,0:T(8,128)S(1)}, u32[]{:S(2)}, u32[]{:S(2)}) collective-permute-start(f32[512,128]{1,0:T(8,128)S(1)} %collective-permute-done.2), channel_id=1, source_target_pairs={{0,1},{1,2},{2,3},{3,4},{4,5},{5,6},{6,7},{7,0},{8,9},{9,10},{10,1... | collective-permute-start | bytes 786440 | tf_op jit(solution)/shard_map/ppermute | solution.py:16
  39.6 7.6 %collective-permute-start.4 = (f32[512,128]{1,0:T(8,128)S(1)}, f32[512,128]{1,0:T(8,128)S(1)}, u32[]{:S(2)}, u32[]{:S(2)}) collective-permute-start(f32[512,128]{1,0:T(8,128)S(1)} %collective-permute-done.3), channel_id=1, source_target_pairs={{0,1},{1,2},{2,3},{3,4},{4,5},{5,6},{6,7},{7,0},{8,9},{9,10},{10,1... | collective-permute-start | bytes 786440 | tf_op jit(solution)/shard_map/ppermute | solution.py:16
  39.6 7.7 %copy-start.3 = (f32[512,128]{1,0:T(8,128)S(1)}, f32[512,128]{1,0:T(8,128)}, u32[]{:S(2)}) copy-start(f32[512,128]{1,0:T(8,128)} %copy-done.2) | copy-start | bytes 786436
  47.2 7.6 %collective-permute-start.5 = (f32[512,128]{1,0:T(8,128)S(1)}, f32[512,128]{1,0:T(8,128)S(1)}, u32[]{:S(2)}, u32[]{:S(2)}) collective-permute-start(f32[512,128]{1,0:T(8,128)S(1)} %collective-permute-done.4), channel_id=1, source_target_pairs={{0,1},{1,2},{2,3},{3,4},{4,5},{5,6},{6,7},{7,0},{8,9},{9,10},{10,1... | collective-permute-start | bytes 786440 | tf_op jit(solution)/shard_map/ppermute | solution.py:16
  54.8 7.6 %collective-permute-start.6 = (f32[512,128]{1,0:T(8,128)S(1)}, f32[512,128]{1,0:T(8,128)S(1)}, u32[]{:S(2)}, u32[]{:S(2)}) collective-permute-start(f32[512,128]{1,0:T(8,128)S(1)} %collective-permute-done.5), channel_id=1, source_target_pairs={{0,1},{1,2},{2,3},{3,4},{4,5},{5,6},{6,7},{7,0},{8,9},{9,10},{10,1... | collective-permute-start | bytes 786440 | tf_op jit(solution)/shard_map/ppermute | solution.py:16
  62.7 2.2 copy-start
  187.9 52.8 %copy-start.4 = (f32[512]{0:T(512)}, f32[512]{0:T(512)S(1)}, u32[]{:S(2)}) copy-start(f32[512]{0:T(512)S(1)} %multiply_subtract_fusion.1) | copy-start | bytes 6148
  206.2 34.4 %copy-start.5 = (f32[512]{0:T(512)}, f32[512]{0:T(512)S(1)}, u32[]{:S(2)}) copy-start(f32[512]{0:T(512)S(1)} %get-tuple-element.4) | copy-start | bytes 6148
  240.7 134.8 %all-reduce.5.cloned.1.call-start = ((), (), s32[]{:S(2)}) async-start(), calls=%async_computation.2 | async-start | bytes 4194304 | tf_op jit(solution)/shard_map/psum | solution.py:78
Sparse Core Ops, SparseCore 0:
  9.8 37.7 all-gather.1
  240.8 62.3 all-reduce.2
  306.3 69.0 all-reduce.4
